TPU v7x, 128 devices: a whole 4x4x4 slice. The times are simulated.
128 devices in a mesh: agent: 8 (over z, core), chan: 8 (over y, x_hi), batch: 2 (over x_lo).
Axes of the slice: x: 4 (x_hi: 2, x_lo: 2; x = x_hi * 2 + x_lo), y: 4, z: 4, core: 2. Of those that a mesh axis runs over, the one named last changes fastest.
Arguments:
- features: bfloat16 [256, 16, 16384], P(None, None, ('agent', 'chan', 'batch')), may hold values from -6 to 6
- norm_gain: float32 [256], replicated, may hold values from 0.1 to 1.9
- tok_in: bfloat16 [16384, 2048], P('agent'), may hold values from -0.046875 to 0.046875
- tok_out: bfloat16 [2048, 16384], P(None, 'agent'), may hold values from -0.125 to 0.125
- mix_gain: float32 [256], replicated, may hold values from 0.1 to 1.9
- chan_in: bfloat16 [256, 1024], replicated, may hold values from -0.375 to 0.375
- chan_out: bfloat16 [1024, 256], replicated, may hold values from -0.1875 to 0.1875
- head: bfloat16 [256, 8], replicated, may hold values from -8 to 8
- actions: int32 [16, 16384], P(None, ('agent', 'chan', 'batch')), may hold values from 0 to 7
- order: int32 [16384], P(('agent', 'chan', 'batch')), may hold values from 0 to 16383, as said below
Outputs:
- input_grad: float32 [256, 16, 16384], P(None, None, ('agent', 'chan', 'batch'))
- head_grad: float32 [256, 8], replicated
Inputs may be any that keep to these rules, and one draw needn't show every extreme that they name: order maps each aligned block of 128 agents one to one onto the same block.
All inputs are finite; a program needn't handle non-finite values.
Results may differ from a plain program's by a relative error of at most 0.025.
Values may be sent and summed in bfloat16 or wider, within the bound.
A program may use at most 128 MiB of HBM per device.

v0:
```python
import jax
import jax.numpy as jnp
from jax import lax
from jax.sharding import PartitionSpec as P

A = 16384


GELU_K = 0.7978845608028654
GELU_C = 0.044715
EPS = 1e-05


def gelu_value(v):
    return 0.5 * v * (1.0 + jnp.tanh(GELU_K * (v + GELU_C * v * v * v)))


def gelu_slope(v):
    inner = jnp.tanh(GELU_K * (v + GELU_C * v * v * v))
    return 0.5 * (1.0 + inner) + 0.5 * v * (1.0 - inner * inner) * GELU_K * (
        1.0 + 3.0 * GELU_C * v * v
    )


def shaped_gain(gain, field):
    return gain.reshape((gain.shape[0],) + (1,) * (field.ndim - 1))


def norm_forward(field, gain):
    center = jnp.mean(field, axis=0, keepdims=True)
    spread = jnp.mean(jnp.square(field - center), axis=0, keepdims=True)
    scale = lax.rsqrt(spread + EPS)
    unit = (field - center) * scale
    return (unit * shaped_gain(gain, field), unit, scale)


def norm_backward(upstream, gain, unit, scale):
    weighted = upstream * shaped_gain(gain, upstream)
    return scale * (
        weighted
        - jnp.mean(weighted, axis=0, keepdims=True)
        - unit * jnp.mean(weighted * unit, axis=0, keepdims=True)
    )


def to_tokens(field):
    return lax.all_to_all(field, ("chan", "batch"), split_axis=0, concat_axis=2, tiled=True)


def to_channels(field):
    return lax.all_to_all(field, ("chan", "batch"), split_axis=2, concat_axis=0, tiled=True)


def project(weight, hidden_dim, rows):
    agent_dim = 1 - hidden_dim
    partial_sum = lax.dot_general(
        weight, rows, (((agent_dim,), (1,)), ((), ())), preferred_element_type=jnp.float32
    )
    return lax.psum(partial_sum, "agent")


def expand(spread, weight, hidden_dim):
    return lax.dot_general(
        spread, weight, (((0,), (hidden_dim,)), ((), ())), preferred_element_type=jnp.float32
    )


def shards(features, norm_gain, tok_in, tok_out, mix_gain, chan_in, chan_out, head, actions, order):
    wide = features.astype(jnp.float32)
    chans, samples, local = wide.shape
    normed_in, unit_in, scale_in = norm_forward(wide, norm_gain)
    spread_in = to_tokens(normed_in.astype(jnp.bfloat16))
    token_chans, _, agents = spread_in.shape
    token_rows = spread_in.reshape(token_chans * samples, agents)
    hidden_pre = project(tok_in, 1, token_rows)
    hidden_act = gelu_value(hidden_pre).astype(jnp.bfloat16)
    mixed = (
        expand(hidden_act, tok_out, 0).astype(jnp.bfloat16).reshape(token_chans, samples, agents)
    )
    mixed_back = to_channels(mixed)
    first = wide + mixed_back.astype(jnp.float32)
    normed_mid, unit_mid, scale_mid = norm_forward(first, mix_gain)
    flat_mid = normed_mid.astype(jnp.bfloat16).reshape(chans, samples * local)
    inner_pre = lax.dot_general(
        chan_in, flat_mid, (((0,), (0,)), ((), ())), preferred_element_type=jnp.float32
    )
    inner = gelu_value(inner_pre).astype(jnp.bfloat16)
    outer = lax.dot_general(
        chan_out, inner, (((0,), (0,)), ((), ())), preferred_element_type=jnp.float32
    )
    second = (first.reshape(chans, samples * local) + outer).astype(jnp.bfloat16)
    logits = lax.dot_general(
        head, second, (((0,), (0,)), ((), ())), preferred_element_type=jnp.float32
    )
    target = jnp.take_along_axis(actions, (order % local)[None, :], axis=1).reshape(
        1, samples * local
    )
    phases = lax.broadcasted_iota(jnp.int32, logits.shape, 0)
    picked = (phases == target).astype(jnp.float32)
    top = jnp.max(logits, axis=0, keepdims=True)
    exps = jnp.exp(logits - top)
    probs = exps / jnp.sum(exps, axis=0, keepdims=True)
    slope = (probs - picked).astype(jnp.bfloat16)
    head_part = lax.dot_general(
        second, slope, (((1,), (1,)), ((), ())), preferred_element_type=jnp.float32
    )
    head_total = lax.psum(head_part, ("agent", "chan", "batch"))
    head_grad = head_total * (1.0 / (samples * A))
    back_second = lax.dot_general(
        head, slope, (((1,), (0,)), ((), ())), preferred_element_type=jnp.float32
    )
    back_low = back_second.astype(jnp.bfloat16)
    back_inner = lax.dot_general(
        chan_out, back_low, (((1,), (0,)), ((), ())), preferred_element_type=jnp.float32
    )
    back_inner_pre = (back_inner * gelu_slope(inner_pre)).astype(jnp.bfloat16)
    back_mid = lax.dot_general(
        chan_in, back_inner_pre, (((1,), (0,)), ((), ())), preferred_element_type=jnp.float32
    )
    back_first = back_second.reshape(chans, samples, local) + norm_backward(
        back_mid.reshape(chans, samples, local), mix_gain, unit_mid, scale_mid
    )
    back_tokens = to_tokens(back_first.astype(jnp.bfloat16))
    back_rows = back_tokens.reshape(token_chans * samples, agents)
    back_hidden = project(tok_out, 0, back_rows)
    back_hidden_pre = (back_hidden * gelu_slope(hidden_pre)).astype(jnp.bfloat16)
    back_spread = (
        expand(back_hidden_pre, tok_in, 1)
        .astype(jnp.bfloat16)
        .reshape(token_chans, samples, agents)
    )
    back_norm = to_channels(back_spread)
    input_grad = back_first + norm_backward(
        back_norm.astype(jnp.float32), norm_gain, unit_in, scale_in
    )
    return (input_grad, head_grad)


def solution(mesh):
    in_specs = (
        P(None, None, ("agent", "chan", "batch")),
        P(),
        P("agent", None),
        P(None, "agent"),
        P(),
        P(),
        P(),
        P(),
        P(None, ("agent", "chan", "batch")),
        P(("agent", "chan", "batch")),
    )
    out_specs = (P(None, None, ("agent", "chan", "batch")), P())
    return jax.shard_map(shards, mesh=mesh, in_specs=in_specs, out_specs=out_specs, check_vma=False)
```

profile of v0, /device:TPU:1, one launch (start us, length us, event | category | flops | bytes accessed | tf_op | source)
XLA Modules:
  0.0 469.6 jit_solution(13224073951282337597)
XLA Ops:
  7.2 1.6 convert_reduce_fusion
  8.9 1.5 fusion.21
  10.4 0.4 fusion.16
  10.8 23.5 %all_to_all.48 = bf16[256,16,128]{2,1,0:T(8,128)(2,1)S(1)} all-to-all(bf16[256,16,128]{2,1,0:T(8,128)(2,1)S(1)} %fusion.16), channel_id=1, replica_groups=mesh['agent'=8,'chan'=8,'batch'=2] {'chan','batch'}, dimensions={0} | all-to-all | bytes 2097152 | tf_op jit(solution)/shard_map/all_to_all | solution.py:47
  34.3 0.7 copy.56
  35.0 7.0 %convolution_bitcast_fusion.1 = f32[2048,256]{0,1:T(8,128)} fusion(bf16[2048,2048]{1,0:T(8,128)(2,1)} %param.12, bf16[32,8,16,128]{3,2,1,0:T(8,128)(2,1)S(1)} %bitcast.134), kind=kOutput, calls=%fused_computation.23 | convolution fusion | flops 2147483648 | bytes 11534336 | tf_op jit(solution)/shard_map/dot_general | solution.py:56
  42.1 64.0 %all-reduce.3.cloned.1.call-done = f32[2048,256]{0,1:T(8,128)} async-done(((f32[2048,256]{0,1:T(8,128)}), f32[2048,256]{0,1:T(8,128)}) %all-reduce.3.cloned.1.call-update) | async-done | bytes 2097168 | tf_op jit(solution)/shard_map/psum | solution.py:59
  106.1 6.6 %convolution_convert_fusion.1 = bf16[256,2048]{1,0:T(8,128)(2,1)S(1)} fusion(bf16[2048,2048]{1,0:T(8,128)(2,1)} %param.13, f32[2048,256]{0,1:T(8,128)} %all-reduce.3.cloned.1.call-done), kind=kOutput, calls=%fused_computation.27 | convolution fusion | flops 2152726528 | bytes 11534336 | tf_op jit(solution)/shard_map/dot_general | solution.py:63
  112.6 8.5 %copy.57 = bf16[16,16,2048]{1,0,2:T(8,128)(2,1)} copy(bf16[16,16,2048]{2,1,0:T(8,128)(2,1)S(1)} %bitcast.133) | data formatting | bytes 2097152 | tf_op jit(solution)/shard_map/reshape | solution.py:78
  121.1 11.2 %reshape.152 = bf16[16,2,16384]{2,1,0:T(2,128)(2,1)} reshape(bf16[2048,16,16]{2,1,0:T(8,128)(2,1)} %bitcast.124) | data formatting | bytes 2097152
  132.4 6.7 %all-to-all-start.1 = ((bf16[16,2,16384]{2,1,0:T(2,128)(2,1)}), bf16[16,2,16384]{2,1,0:T(2,128)(2,1)S(1)}, u32[]{:S(2)}, u32[]{:S(2)}) async-start(bf16[16,2,16384]{2,1,0:T(2,128)(2,1)} %reshape.152), calls=%async_computation.1 | async-start | bytes 2097152 | tf_op jit(solution)/shard_map/all_to_all | solution.py:51
  139.4 0.6 gather_fusion
  140.2 13.4 %all-to-all-done.1 = bf16[16,2,16384]{2,1,0:T(2,128)(2,1)S(1)} async-done(((bf16[16,2,16384]{2,1,0:T(2,128)(2,1)}), bf16[16,2,16384]{2,1,0:T(2,128)(2,1)S(1)}, u32[]{:S(2)}, u32[]{:S(2)}) %all-to-all-start.1) | async-done | bytes 1048608 | tf_op jit(solution)/shard_map/all_to_all | solution.py:51
  153.6 7.5 %reshape.153 = bf16[2048,16,16]{2,1,0:T(8,128)(2,1)} reshape(bf16[16,2,16384]{2,1,0:T(2,128)(2,1)S(1)} %all-to-all-done.1) | data formatting | bytes 2097152
  161.1 10.9 %convert_bitcast_fusion = f32[16,16,16,128]{2,1,3,0:T(8,128)} fusion(bf16[16,16,16,128]{1,0,3,2:T(8,128)(2,1)} %bitcast.123), kind=kLoop, calls=%fused_computation.1 | loop fusion | flops 524288 | bytes 3145728 | tf_op jit(solution)/shard_map/convert_element_type | solution.py:81
  172.0 11.4 %copy.58 = f32[16,16,16,128]{3,2,1,0:T(8,128)} copy(f32[16,16,16,128]{2,1,3,0:T(8,128)} %convert_bitcast_fusion) | data formatting | bytes 4194304 | tf_op jit(solution)/shard_map/convert_element_type | solution.py:81
  183.4 2.2 fusion.76
  185.6 1.8 copy.59
  187.4 0.3 multiply_reduce_fusion.2
  187.7 0.4 copy-done.13
  188.1 0.4 multiply_convert_fusion.8
  188.5 1.3 fusion.34
  190.2 3.0 fusion.10
  193.2 0.4 fusion.77
  193.6 0.6 copy-done.8
  194.2 1.8 fusion.71
  196.0 9.5 %fusion.29 = (f32[2048]{0:T(1024)S(1)}, f32[2048,256]{1,0:T(8,128)}) fusion(f32[256]{0:T(256)S(1)} %copy-done.13, bf16[256,1024]{1,0:T(8,128)(2,1)S(1)} %copy-done, f32[2048,1024]{1,0:T(8,128)} %copy-done.6, bf16[1024,256]{1,0:T(8,128)(2,1)S(1)} %copy-done.15, f32[2048,256]{1,0:T(8,128)} %fusion.71), kind=kOutput, calls=%fused_computation.48 | convolution fusion | flops 2188376064 | bytes 13640704 | tf_op jit(solution)/shard_map/dot_general | solution.py:117
  205.6 3.1 copy.62
  208.6 3.2 copy.63
  211.9 2.1 multiply_reduce_fusion.1
  214.1 0.6 copy-done.7
  214.7 2.1 fusion.75
  216.8 17.1 %all_to_all.49 = bf16[256,16,128]{2,1,0:T(8,128)(2,1)S(1)} all-to-all(bf16[256,16,128]{2,1,0:T(8,128)(2,1)S(1)} %get-tuple-element.2), channel_id=1, replica_groups=mesh['agent'=8,'chan'=8,'batch'=2] {'chan','batch'}, dimensions={0} | all-to-all | bytes 2097152 | tf_op jit(solution)/shard_map/all_to_all | solution.py:47
  233.9 0.7 copy.64
  234.6 7.0 %convolution_bitcast_fusion = f32[2048,256]{0,1:T(8,128)} fusion(bf16[2048,2048]{1,0:T(8,128)(2,1)} %param.13, bf16[32,8,16,128]{3,2,1,0:T(8,128)(2,1)S(1)} %bitcast.135), kind=kOutput, calls=%fused_computation.22 | convolution fusion | flops 2147483648 | bytes 11534336 | tf_op jit(solution)/shard_map/dot_general | solution.py:56
  241.6 70.6 %all-reduce.5.cloned.1.call-done = f32[2048,256]{0,1:T(8,128)} async-done(((f32[2048,256]{0,1:T(8,128)}), f32[2048,256]{0,1:T(8,128)}) %all-reduce.5.cloned.1.call-update) | async-done | bytes 2097168 | tf_op jit(solution)/shard_map/psum | solution.py:59
  312.3 7.8 %convolution_convert_fusion = bf16[256,2048]{1,0:T(8,128)(2,1)S(1)} fusion(bf16[2048,2048]{1,0:T(8,128)(2,1)} %param.12, f32[2048,256]{0,1:T(8,128)} %all-reduce.5.cloned.1.call-done, f32[2048,256]{0,1:T(8,128)} %all-reduce.3.cloned.1.call-done), kind=kOutput, calls=%fused_computation.26 | convolution fusion | flops 2157969408 | bytes 13631488 | tf_op jit(solution)/shard_map/dot_general | solution.py:63
  320.1 8.5 %copy.65 = bf16[16,16,2048]{1,0,2:T(8,128)(2,1)} copy(bf16[16,16,2048]{2,1,0:T(8,128)(2,1)S(1)} %bitcast.132) | data formatting | bytes 2097152 | tf_op jit(solution)/shard_map/reshape | solution.py:130
  328.6 11.2 %reshape.154 = bf16[16,2,16384]{2,1,0:T(2,128)(2,1)} reshape(bf16[2048,16,16]{2,1,0:T(8,128)(2,1)} %bitcast.125) | data formatting | bytes 2097152
  339.9 6.7 %all-to-all-start.3 = ((bf16[16,2,16384]{2,1,0:T(2,128)(2,1)}), bf16[16,2,16384]{2,1,0:T(2,128)(2,1)S(1)}, u32[]{:S(2)}, u32[]{:S(2)}) async-start(bf16[16,2,16384]{2,1,0:T(2,128)(2,1)} %reshape.154), calls=%async_computation.3 | async-start | bytes 2097152 | tf_op jit(solution)/shard_map/all_to_all | solution.py:51
  346.9 73.3 %psum.23 = f32[256,8]{0,1:T(8,128)S(1)} all-reduce(f32[256,8]{0,1:T(8,128)S(1)} %fusion.69), channel_id=1, replica_groups=mesh['agent'=8,'chan'=8,'batch'=2] {'agent','chan','batch'}, use_global_device_ids=true, to_apply=%region_12.13 | all-reduce | flops 2048 | bytes 16384 | tf_op jit(solution)/shard_map/psum | solution.py:107
  420.1 0.6 broadcast_multiply_fusion
  420.7 7.5 %reshape.155 = bf16[2048,16,16]{2,1,0:T(8,128)(2,1)} reshape(bf16[16,2,16384]{2,1,0:T(2,128)(2,1)S(1)} %all-to-all-done.3) | data formatting | bytes 2097152
  428.3 10.9 %convert_bitcast_fusion.1 = f32[16,16,16,128]{2,1,3,0:T(8,128)} fusion(bf16[2048,16,16]{2,1,0:T(8,128)(2,1)} %reshape.155), kind=kLoop, calls=%fused_computation.2 | loop fusion | flops 524288 | bytes 3145728 | tf_op jit(solution)/shard_map/convert_element_type | solution.py:134
  439.2 5.7 %multiply_reduce_fusion = f32[16,128]{0,1:T(8,128)S(1)} fusion(f32[16,16]{1,0:T(8,128)S(1)} %mul.242, bf16[16,16,16,128]{1,0,3,2:T(8,128)(2,1)} %bitcast.122), kind=kLoop, calls=%fused_computation.3 | loop fusion | flops 1570816 | bytes 1057792 | tf_op jit(solution)/shard_map/reduce_sum | solution.py:41
  444.9 11.5 %copy.66 = f32[16,16,16,128]{3,2,1,0:T(8,128)} copy(f32[16,16,16,128]{2,1,3,0:T(8,128)} %convert_bitcast_fusion.1) | data formatting | bytes 4194304 | tf_op jit(solution)/shard_map/convert_element_type | solution.py:134
  456.5 2.2 fusion.17
  458.7 3.6 fusion.20
  (52 shorter events, 1.4 us)
Async XLA Ops:
  7.2 181.3 %copy-start = (bf16[256,1024]{1,0:T(8,128)(2,1)S(1)}, bf16[256,1024]{1,0:T(8,128)(2,1)}, u32[]{:S(2)}) copy-start(bf16[256,1024]{1,0:T(8,128)(2,1)} %param.15) | copy-start | bytes 1572868
  7.2 3.2 copy-start.2
  7.2 3.2 copy-start.12
  7.2 98.9 %all-reduce.3.cloned.1.call-start = ((), (), s32[]{:S(2)}) async-start(), calls=%async_computation.4 | async-start | bytes 4194304 | tf_op jit(solution)/shard_map/psum | solution.py:59
  132.4 6.9 %copy-start.14 = (s32[16,128]{1,0:T(8,128)S(1)}, s32[16,128]{1,0:T(8,128)}, u32[]{:S(2)}) copy-start(s32[16,128]{1,0:T(8,128)} %param.18) | copy-start | bytes 24580
  132.4 7.0 %copy-start.16 = (s32[128]{0:T(128)S(1)}, s32[128]{0:T(128)}, u32[]{:S(2)}) copy-start(s32[128]{0:T(128)} %param.19) | copy-start | bytes 1540
  132.4 21.2 %all-to-all-start.1 = ((bf16[16,2,16384]{2,1,0:T(2,128)(2,1)}), bf16[16,2,16384]{2,1,0:T(2,128)(2,1)S(1)}, u32[]{:S(2)}, u32[]{:S(2)}) async-start(bf16[16,2,16384]{2,1,0:T(2,128)(2,1)} %reshape.152), calls=%async_computation.1 | async-start | bytes 2097152 | tf_op jit(solution)/shard_map/all_to_all | solution.py:51
  139.1 173.2 %all-reduce.5.cloned.1.call-start = ((), (), s32[]{:S(2)}) async-start(), calls=%async_computation.5 | async-start | bytes 4194304 | tf_op jit(solution)/shard_map/psum | solution.py:59
  187.4 0.7 copy-start.13
  188.5 1.6 copy-start.10
  188.5 1.7 copy-start.15
  189.8 3.3 copy-start.6
  190.2 3.0 copy-start.11
  193.2 1.0 copy-start.8
  211.9 2.2 copy-start.4
  211.9 2.8 copy-start.7
  339.9 6.7 %copy-start.9 = (bf16[256,2048]{0,1:T(8,128)(2,1)S(1)}, bf16[256,2048]{0,1:T(8,128)(2,1)}, u32[]{:S(2)}) copy-start(bf16[256,2048]{0,1:T(8,128)(2,1)} %copy-done.8) | copy-start | bytes 3145732
  339.9 80.9 %all-to-all-start.3 = ((bf16[16,2,16384]{2,1,0:T(2,128)(2,1)}), bf16[16,2,16384]{2,1,0:T(2,128)(2,1)S(1)}, u32[]{:S(2)}, u32[]{:S(2)}) async-start(bf16[16,2,16384]{2,1,0:T(2,128)(2,1)} %reshape.154), calls=%async_computation.3 | async-start | bytes 2097152 | tf_op jit(solution)/shard_map/all_to_all | solution.py:51
  444.9 11.5 %copy-start.3 = (bf16[256,16,128]{2,1,0:T(8,128)(2,1)S(1)}, bf16[256,16,128]{2,1,0:T(8,128)(2,1)}, u32[]{:S(2)}) copy-start(bf16[256,16,128]{2,1,0:T(8,128)(2,1)} %param.10) | copy-start | bytes 3145732
  456.5 2.2 copy-start.5
  458.6 3.6 copy-start.1
Sparse Core Ops, SparseCore 0:
  42.2 63.8 all-reduce.2
  241.8 70.4 all-reduce.4
where the time goes:
time: 477 us; the launch traced here: 470 us
  waiting for transfers between devices  148 us (31%)
  blocking collectives  114 us (24%)
  local copies, waits for them, and re-layouts  89.9 us (19%)
  matrix products  44.8 us (9%)
  other arithmetic  44.6 us (9%)
  between operations  14.8 us (3%)
  starting transfers between devices  13.6 us (3%)
    psum x2, waiting for transfers between devices, project(): return lax.psum(partial_sum, 'agent')  135 us
    psum x1, blocking collectives, shards(): head_total = lax.psum(head_part, ('agent', 'chan', 'batch'))  73.3 us
    all_to_all x2, blocking collectives, to_tokens(): lax.all_to_all(field, ('chan', 'batch'), split_axis=0, concat_axis=2, til...  40.6 us
    unnamed x39, local copies, waits for them, and re-layouts  39.6 us
    dot_general x2, matrix products, expand(): lax.dot_general(spread, weight, (((0,), (hidden_dim,)), ((), ())), prefer...  14.4 us
    dot_general x2, matrix products, project(): lax.dot_general(weight, rows, (((agent_dim,), (1,)), ((), ())), preferred...  14.1 us
    all_to_all x2, waiting for transfers between devices, to_channels(): lax.all_to_all(field, ('chan', 'batch'), split_axis=2, concat_axis=0, til...  13.4 us
    all_to_all x2, starting transfers between devices, to_channels(): lax.all_to_all(field, ('chan', 'batch'), split_axis=2, concat_axis=0, til...  13.3 us
  transfers between devices with their start and end apart: 4, of which 3 were waited for; matrix products, arithmetic and copies ran while one was open for 0% of the time, Pallas kernels for 0%

commit v1 on v0

v1 whole, which is shorter than its diff:
```python
import jax
import jax.numpy as jnp
from jax import lax
from jax.experimental import pallas as pl
from jax.experimental.pallas import tpu as pltpu
from jax.sharding import PartitionSpec as P

MESH = pl.DeviceIdType.MESH
F32 = jnp.float32
BF16 = jnp.bfloat16

A = 16384
B = 16
C = 256
L = 128
NP = 16
CL = C // NP
T = NP * L
J = 2048
K = 1024
NC = 2
NB = B // NC
R = NB * CL
Q = J // 8

GELU_K = 0.7978845608028654
GELU_C = 0.044715
EPS = 1e-05


def mm(a, b):
    return lax.dot_general(a, b, (((1,), (0,)), ((), ())), preferred_element_type=F32)


def mm_nt(a, b):
    return lax.dot_general(a, b, (((1,), (1,)), ((), ())), preferred_element_type=F32)


def gelu_both(v):
    square = v * v
    inner = jnp.tanh(v * (GELU_K + (GELU_K * GELU_C) * square))
    half = 0.5 + 0.5 * inner
    value = v * half
    slope = half + (0.5 * v) * (1.0 - inner * inner) * (GELU_K + (3.0 * GELU_K * GELU_C) * square)
    return value, slope


def mean0(v):
    return jnp.sum(v, axis=0, keepdims=True) * (1.0 / C)


def kernel(
    x_hbm, gin_ref, win_hbm, wout_hbm, gmid_ref, ci_hbm, co_hbm, head_ref, act_ref, ord_ref,
    out_hbm, hg_ref,
    x_s, win, wout, ci, co, cit, cot, gin, gmid, head16, headc, tgt, mu, rstd, bf,
    send1, send2, send3, send4, recv1, recv2, recv3, recv4,
    part1, part2, sibr1, sibr2, zs1, zs2, zr1, zr2, hact1, hact2, ownp, hslope,
    inner_s, slope_s, bip_s, hp, hbuf_a, hbuf_y, hbuf_x, hsend,
    ld_sem, out_sem, a2a_s, a2a_r, sib_s, sib_r, z_s, z_r, ag_s, ag_r, fw_s, fw_r,
    ha_s, ha_r, hy_s, hy_r, hx_s, hx_r,
):
    ag = lax.axis_index("agent")
    chan = lax.axis_index("chan")
    batch = lax.axis_index("batch")
    me = chan * 2 + batch
    z = ag // 2
    core = lax.rem(ag, 2)
    y = me // 4
    xx = lax.rem(me, 4)
    mine = core * 4 + z

    def plane(p):
        return {"agent": ag, "chan": p // 2, "batch": lax.rem(p, 2)}

    def line(zz, cc):
        return {"agent": zz * 2 + cc, "chan": chan, "batch": batch}

    def xor(a, d):
        out = a
        if d & 1:
            out = out + 1 - 2 * lax.rem(out, 2)
        if d & 2:
            out = lax.rem(out + 2, 4)
        return out

    loads = [
        pltpu.make_async_copy(x_hbm, x_s, ld_sem.at[0]),
        pltpu.make_async_copy(win_hbm, win, ld_sem.at[1]),
        pltpu.make_async_copy(ci_hbm, ci, ld_sem.at[2]),
        pltpu.make_async_copy(co_hbm, co, ld_sem.at[3]),
        pltpu.make_async_copy(wout_hbm, wout, ld_sem.at[4]),
    ]
    for load in loads:
        load.start()

    barrier = pltpu.get_barrier_semaphore()
    for i in range(1, NP):
        pl.semaphore_signal(barrier, inc=1, device_id=plane(lax.rem(me + i, NP)), device_id_type=MESH)
    for i in range(1, 8):
        pl.semaphore_signal(
            barrier, inc=1,
            device_id={"agent": lax.rem(ag + i, 8), "chan": chan, "batch": batch},
            device_id_type=MESH,
        )

    gin[...] = jnp.transpose(jnp.broadcast_to(gin_ref[...], (L, C)))
    gmid[...] = jnp.transpose(jnp.broadcast_to(gmid_ref[...], (L, C)))
    head_rows = jnp.concatenate([head_ref[...].astype(F32), jnp.zeros((8, C), F32)], axis=0)
    head16[...] = head_rows.astype(BF16)
    wide_head = jnp.concatenate([head_rows, jnp.zeros((L - 16, C), F32)], axis=0)
    headc[...] = jnp.transpose(wide_head)[:, :16].astype(BF16)
    spot = lax.broadcasted_iota(jnp.int32, (L, L), 0) == lax.rem(ord_ref[...], L)
    targets = mm(act_ref[...].astype(F32).astype(BF16), spot.astype(F32).astype(BF16))
    for b in range(B):
        tgt[b] = targets[b : b + 1, :]
    hp[...] = jnp.zeros((16, C), F32)

    def a2a_copy(k, h, send, recv, p, slot):
        return pltpu.make_async_remote_copy(
            src_ref=send.at[p, pl.ds(h * NB, NB)],
            dst_ref=recv.at[h, slot],
            send_sem=a2a_s.at[k, h, p],
            recv_sem=a2a_r.at[k, h, slot],
            device_id=plane(p),
            device_id_type=MESH,
        )

    def a2a_send(k, h, send, recv):
        def body(i, carry):
            a2a_copy(k, h, send, recv, lax.rem(me + i, NP), me).start()
            return carry

        lax.fori_loop(1, NP, body, 0)

    def a2a_wait(k, h, send, recv):
        recv[h, me] = send[me, pl.ds(h * NB, NB)]

        def body(i, carry):
            p = lax.rem(me + i, NP)
            a2a_copy(k, h, send, recv, p, p).wait_recv()
            return carry

        lax.fori_loop(1, NP, body, 0)

    def a2a_drain(k, h, send, recv):
        def body(i, carry):
            a2a_copy(k, h, send, recv, lax.rem(me + i, NP), me).wait_send()
            return carry

        lax.fori_loop(1, NP, body, 0)

    def sib_copy(s, h, part, sibr, i):
        return pltpu.make_async_remote_copy(
            src_ref=part.at[h, i], dst_ref=sibr.at[h, i],
            send_sem=sib_s.at[s, h, i], recv_sem=sib_r.at[s, h, i],
            device_id=line(z, 1 - core), device_id_type=MESH,
        )

    def z_copy(s, h, zs, zr, src, zz, slot):
        return pltpu.make_async_remote_copy(
            src_ref=zs.at[h, src], dst_ref=zr.at[h, slot],
            send_sem=z_s.at[s, h, src], recv_sem=z_r.at[s, h, slot],
            device_id=line(zz, core), device_id_type=MESH,
        )

    def ag_copy(s, h, hact, d, block):
        return pltpu.make_async_remote_copy(
            src_ref=hact.at[h, block], dst_ref=hact.at[h, block],
            send_sem=ag_s.at[s, h, d - 1], recv_sem=ag_r.at[s, h, d - 1],
            device_id=line(xor(z, d), core), device_id_type=MESH,
        )

    def fw_copy(s, h, hact, zz, cc):
        return pltpu.make_async_remote_copy(
            src_ref=hact.at[h, cc * 4 + zz], dst_ref=hact.at[h, cc * 4 + zz],
            send_sem=fw_s.at[s, h, zz], recv_sem=fw_r.at[s, h, zz],
            device_id=line(z, 1 - core), device_id_type=MESH,
        )

    def rows_of(recv, h):
        return jnp.concatenate([recv[h, p].reshape(R, L) for p in range(NP)], axis=1)

    def contract(s, h, recv, product, part, sibr, zs, zr):
        def for_sibling(i, carry):
            part[h, i] = product(rows_of(recv, h), (1 - core) * 4 + 2 * i).astype(BF16)
            sib_copy(s, h, part, sibr, i).start()
            return carry

        lax.fori_loop(0, 2, for_sibling, 0)
        half = z // 2
        other = 1 - half
        far = product(rows_of(recv, h), core * 4 + 2 * other)
        sib_copy(s, h, part, sibr, other).wait_recv()
        far = far + sibr[h, other].astype(F32)
        zs[h, 0] = far[:, :Q].astype(BF16)
        zs[h, 1] = far[:, Q:].astype(BF16)
        low = lax.rem(z, 2)
        z_copy(s, h, zs, zr, low, xor(z, 2), 1).start()
        z_copy(s, h, zs, zr, 1 - low, xor(z, 3), 2).start()
        near = product(rows_of(recv, h), core * 4 + 2 * half)
        sib_copy(s, h, part, sibr, half).wait_recv()
        near = near + sibr[h, half].astype(F32)
        ownp[s, h, 0] = near[:, :Q]
        ownp[s, h, 1] = near[:, Q:]
        zs[h, 2] = ownp[s, h, 1 - low].astype(BF16)
        z_copy(s, h, zs, zr, 2, xor(z, 1), 0).start()

    def summed(s, h, zs, zr):
        low = lax.rem(z, 2)
        total = ownp[s, h, low]
        for d in range(1, 4):
            z_copy(s, h, zs, zr, 0, xor(z, d), d - 1).wait_recv()
            total = total + zr[h, d - 1].astype(F32)
        return total

    def spread(s, h, hact):
        for d in range(1, 4):
            ag_copy(s, h, hact, d, mine).start()
        fw_copy(s, h, hact, z, core).start()

    def forward(s, h, hact):
        for d in (1, 3, 2):
            zz = xor(z, d)
            ag_copy(s, h, hact, d, core * 4 + zz).wait_recv()
            fw_copy(s, h, hact, zz, core).start()

    def gather_wait(s, h, hact):
        for zz in range(4):
            fw_copy(s, h, hact, zz, 1 - core).wait_recv()

    def expand(k, h, hact, product, send, recv):
        def store(tile, group):
            for i in range(4):
                send[group * 4 + i, pl.ds(h * NB, NB)] = tile[:, i * L : (i + 1) * L].reshape(NB, CL, L)

        def row_of(group):
            rows = jnp.concatenate([hact[h, q] for q in range(8)], axis=1)
            store(product(rows, group).astype(BF16), group)

        def body(t, carry):
            group = lax.rem(y + 1 + t, 4)
            row_of(group)
            for i in range(4):
                p = group * 4 + lax.rem(xx + i, 4)
                a2a_copy(k, h, send, recv, p, me).start()
            return carry

        lax.fori_loop(0, 3, body, 0)
        row_of(y)
        for i in range(1, 4):
            a2a_copy(k, h, send, recv, y * 4 + lax.rem(xx + i, 4), me).start()

    def cols(w, block):
        return w[:, pl.ds(pl.multiple_of(block * Q, Q), 2 * Q)]

    def rows(w, block):
        return w[pl.ds(pl.multiple_of(block * Q, Q), 2 * Q), :]

    def norm_in(h):
        def body(i, carry):
            b = h * NB + i
            field = x_s[b].astype(F32)
            center = mean0(field)
            field = field - center
            scale = lax.rsqrt(mean0(field * field) + EPS)
            mu[b] = center
            rstd[b] = scale
            send1[:, b] = (field * scale * gin[...]).astype(BF16).reshape(NP, CL, L)
            return carry

        lax.fori_loop(0, NB, body, 0)

    def channel_part(h):
        def body(i, carry):
            l0, l1 = 2 * i, 2 * i + 1
            b0, b1 = h * NB + l0, h * NB + l1
            wide = jnp.concatenate([x_s[b0], x_s[b1]], axis=1).astype(F32)
            mixed = jnp.concatenate([recv2[h, :, l0].reshape(C, L), recv2[h, :, l1].reshape(C, L)], axis=1)
            first = wide + mixed.astype(F32)
            gain = jnp.concatenate([gmid[...], gmid[...]], axis=1)
            center = mean0(first)
            unit = first - center
            scale = lax.rsqrt(mean0(unit * unit) + EPS)
            unit = unit * scale
            normed = (unit * gain).astype(BF16)
            for kb in range(4):
                block = slice(kb * 256, kb * 256 + 256)
                value, slope = gelu_both(mm(cit[block, :], normed))
                inner_s[block, :] = value.astype(BF16)
                slope_s[block, :] = slope
            second = (first + mm(cot[...], inner_s[...])).astype(BF16)
            logits = mm(head16[...], second)[:8]
            target = jnp.concatenate([tgt[b0], tgt[b1]], axis=1)
            phases = lax.broadcasted_iota(jnp.int32, (8, 2 * L), 0).astype(F32)
            exps = jnp.exp(logits - jnp.max(logits, axis=0, keepdims=True))
            probs = exps / jnp.sum(exps, axis=0, keepdims=True)
            diff = probs - jnp.where(phases == target, 1.0, 0.0)
            slope16 = jnp.concatenate([diff, jnp.zeros((8, 2 * L), F32)], axis=0).astype(BF16)
            hp[...] += mm_nt(slope16, second)
            back_second = mm(headc[...], slope16)
            back_low = back_second.astype(BF16)
            for kb in range(4):
                block = slice(kb * 256, kb * 256 + 256)
                bip_s[block, :] = (mm(co[block, :], back_low) * slope_s[block, :]).astype(BF16)
            w = mm(ci[...], bip_s[...]) * gain
            back = back_second + scale * (w - mean0(w) - unit * mean0(w * unit))
            bf[b0] = back[:, :L]
            bf[b1] = back[:, L:]
            low = back.astype(BF16)
            send3[:, b0] = low[:, :L].reshape(NP, CL, L)
            send3[:, b1] = low[:, L:].reshape(NP, CL, L)
            return carry

        lax.fori_loop(0, NB // 2, body, 0)

    def norm_back(h):
        def body(i, carry):
            b = h * NB + i
            scale = rstd[b]
            unit = (x_s[b].astype(F32) - mu[b]) * scale
            w = recv4[h, :, i].reshape(C, L).astype(F32) * gin[...]
            bf[b] = bf[b] + scale * (w - mean0(w) - unit * mean0(w * unit))
            return carry

        lax.fori_loop(0, NB, body, 0)

    def out_copy(h):
        piece = pl.ds(h * NB, NB)
        return pltpu.make_async_copy(bf.at[piece], out_hbm.at[piece], out_sem.at[h])

    def ha_copy(i):
        return pltpu.make_async_remote_copy(
            src_ref=hsend.at[0], dst_ref=hbuf_a.at[ag], send_sem=ha_s.at[i], recv_sem=ha_r.at[i],
            device_id={"agent": lax.rem(ag + i, 8), "chan": chan, "batch": batch}, device_id_type=MESH,
        )

    def hy_copy(i):
        return pltpu.make_async_remote_copy(
            src_ref=hsend.at[1], dst_ref=hbuf_y.at[y], send_sem=hy_s.at[i], recv_sem=hy_r.at[i],
            device_id=plane(lax.rem(y + i, 4) * 4 + xx), device_id_type=MESH,
        )

    def hx_copy(i):
        return pltpu.make_async_remote_copy(
            src_ref=hsend.at[2], dst_ref=hbuf_x.at[xx], send_sem=hx_s.at[i], recv_sem=hx_r.at[i],
            device_id=plane(y * 4 + lax.rem(xx + i, 4)), device_id_type=MESH,
        )

    def total(buf, n):
        out = buf[0]
        for i in range(1, n):
            out = out + buf[i]
        return out

    loads[0].wait()
    norm_in(0)
    pl.semaphore_wait(barrier, NP - 1 + 7)
    a2a_send(0, 0, send1, recv1)
    for h in range(1, NC):
        norm_in(h)
        a2a_send(0, h, send1, recv1)
    loads[2].wait()
    loads[3].wait()
    for kb in range(4):
        block = slice(kb * 256, kb * 256 + 256)
        cit[block, :] = jnp.transpose(ci[:, block])
        cot[:, block] = jnp.transpose(co[block, :])
    loads[1].wait()
    for h in range(NC):
        a2a_wait(0, h, send1, recv1)
        contract(0, h, recv1, lambda a, block: mm(a, cols(win, block)), part1, sibr1, zs1, zr1)
    for h in range(NC):
        value, slope = gelu_both(summed(0, h, zs1, zr1))
        hact1[h, mine] = value.astype(BF16)
        hslope[h] = slope
        spread(0, h, hact1)
    loads[4].wait()
    for h in range(NC):
        forward(0, h, hact1)
        gather_wait(0, h, hact1)
        expand(1, h, hact1, lambda a, group: mm(a, cols(wout, group * 2)), send2, recv2)
    for h in range(NC):
        a2a_wait(1, h, send2, recv2)
        channel_part(h)
        a2a_send(2, h, send3, recv3)
    hsend[0] = hp[:8]
    hbuf_a[ag] = hp[:8]
    for i in range(1, 8):
        ha_copy(i).start()
    for h in range(NC):
        a2a_wait(2, h, send3, recv3)
        contract(1, h, recv3, lambda a, block: mm_nt(a, rows(wout, block)), part2, sibr2, zs2, zr2)
    for i in range(1, 8):
        ha_copy(i).wait()
    sums = total(hbuf_a, 8)
    hsend[1] = sums
    hbuf_y[y] = sums
    for i in range(1, 4):
        hy_copy(i).start()
    for h in range(NC):
        hact2[h, mine] = (summed(1, h, zs2, zr2) * hslope[h]).astype(BF16)
        spread(1, h, hact2)
    for i in range(1, 4):
        hy_copy(i).wait()
    sums = total(hbuf_y, 4)
    hsend[2] = sums
    hbuf_x[xx] = sums
    for i in range(1, 4):
        hx_copy(i).start()
    for h in range(NC):
        forward(1, h, hact2)
        gather_wait(1, h, hact2)
        expand(3, h, hact2, lambda a, group: mm_nt(a, rows(win, group * 2)), send4, recv4)
    for i in range(1, 4):
        hx_copy(i).wait()
    hg_ref[...] = total(hbuf_x, 4) * (1.0 / (B * A))
    for h in range(NC):
        a2a_wait(3, h, send4, recv4)
        norm_back(h)
        out_copy(h).start()

    for h in range(NC):
        for k, (send, recv) in enumerate(((send1, recv1), (send2, recv2), (send3, recv3), (send4, recv4))):
            a2a_drain(k, h, send, recv)
        for s, (part, sibr, zs, zr, hact) in enumerate(
            ((part1, sibr1, zs1, zr1, hact1), (part2, sibr2, zs2, zr2, hact2))
        ):
            for i in range(2):
                sib_copy(s, h, part, sibr, i).wait_send()
            for i in range(3):
                z_copy(s, h, zs, zr, i, xor(z, 1), 0).wait_send()
            for d in range(1, 4):
                ag_copy(s, h, hact, d, mine).wait_send()
            for zz in range(4):
                fw_copy(s, h, hact, zz, core).wait_send()
        out_copy(h).wait()


def fused(x, gin, win, wout, gmid, ci, co, head, actions, order):
    hbm = pl.BlockSpec(memory_space=pl.ANY)
    vmem = pl.BlockSpec(memory_space=pltpu.VMEM)
    dma = pltpu.SemaphoreType.DMA
    V = pltpu.VMEM
    exchange = V((NP, B, CL, L), BF16)
    arrive = V((NC, NP, NB, CL, L), BF16)
    scratch = [
        V((B, C, L), BF16), V((T, J), BF16), V((J, T), BF16),
        V((C, K), BF16), V((K, C), BF16), V((K, C), BF16), V((C, K), BF16),
        V((C, L), F32), V((C, L), F32), V((16, C), BF16), V((C, 16), BF16),
        V((B, 1, L), F32), V((B, 1, L), F32), V((B, 1, L), F32), V((B, C, L), F32),
        exchange, exchange, exchange, exchange, arrive, arrive, arrive, arrive,
        V((NC, 2, R, 2 * Q), BF16), V((NC, 2, R, 2 * Q), BF16),
        V((NC, 2, R, 2 * Q), BF16), V((NC, 2, R, 2 * Q), BF16),
        V((NC, 3, R, Q), BF16), V((NC, 3, R, Q), BF16),
        V((NC, 3, R, Q), BF16), V((NC, 3, R, Q), BF16),
        V((NC, 8, R, Q), BF16), V((NC, 8, R, Q), BF16),
        V((2, NC, 2, R, Q), F32), V((NC, R, Q), F32),
        V((K, 2 * L), BF16), V((K, 2 * L), F32), V((K, 2 * L), BF16), V((16, C), F32),
        V((8, 8, C), F32), V((4, 8, C), F32), V((4, 8, C), F32), V((3, 8, C), F32),
        dma((5,)), dma((NC,)), dma((4, NC, NP)), dma((4, NC, NP)),
        dma((2, NC, 2)), dma((2, NC, 2)), dma((2, NC, 3)), dma((2, NC, 3)),
        dma((2, NC, 3)), dma((2, NC, 3)), dma((2, NC, 4)), dma((2, NC, 4)),
        dma((8,)), dma((8,)), dma((4,)), dma((4,)), dma((4,)), dma((4,)),
    ]
    return pl.pallas_call(
        kernel,
        out_shape=(jax.ShapeDtypeStruct((B, C, L), F32), jax.ShapeDtypeStruct((8, C), F32)),
        in_specs=[hbm, vmem, hbm, hbm, vmem, hbm, hbm, vmem, vmem, vmem],
        out_specs=(hbm, vmem),
        scratch_shapes=scratch,
        compiler_params=pltpu.CompilerParams(
            collective_id=0, has_side_effects=True, vmem_limit_bytes=58 << 20
        ),
    )(x, gin, win, wout, gmid, ci, co, head, actions, order)


def shards(features, norm_gain, tok_in, tok_out, mix_gain, chan_in, chan_out, head, actions, order):
    grad, head_grad = fused(
        jnp.transpose(features, (1, 0, 2)),
        norm_gain.reshape(1, C),
        tok_in,
        tok_out,
        mix_gain.reshape(1, C),
        chan_in,
        chan_out,
        head.T,
        actions,
        order.reshape(1, L),
    )
    return jnp.transpose(grad, (1, 0, 2)), head_grad.T


def solution(mesh):
    in_specs = (
        P(None, None, ("agent", "chan", "batch")),
        P(),
        P("agent", None),
        P(None, "agent"),
        P(),
        P(),
        P(),
        P(),
        P(None, ("agent", "chan", "batch")),
        P(("agent", "chan", "batch")),
    )
    out_specs = (P(None, None, ("agent", "chan", "batch")), P())
    return jax.shard_map(shards, mesh=mesh, in_specs=in_specs, out_specs=out_specs, check_vma=False)
```

time: 477 us -> 115 us (0.24); the launches traced: 470 us -> 114 us
  waiting for transfers between devices: 148 us -> 0 us
  blocking collectives: 114 us -> 0 us
  Pallas kernels: 0 us -> 106 us
  local copies, waits for them, and re-layouts: 89.9 us -> 7.89 us
  matrix products: 44.8 us -> 0 us
  other arithmetic: 44.6 us -> 0 us
  between operations: 14.8 us -> 0.64 us
  starting transfers between devices: 13.6 us -> 0 us
    psum x2 -> x0, waiting for transfers between devices: 135 us -> none  [project(): return lax.psum(partial_sum, 'agent')]
    pallas_call x0 -> x1, Pallas kernels: none -> 106 us  [fused(): pl.pallas_call(kernel, out_shape=(jax.ShapeDtypeStruct((B, C, L), F32), j...]
    psum x1 -> x0, blocking collectives: 73.3 us -> none  [shards(): head_total = lax.psum(head_part, ('agent', 'chan', 'batch'))]
    dot_general x10 -> x0, matrix products: 44.8 us -> none  [the longest x2 14.4 us: expand(): lax.dot_general(spread, weight, (((0,), (hidden_dim,)), ((), ())), prefer...]
    all_to_all x2 -> x0, blocking collectives: 40.6 us -> none  [to_tokens(): lax.all_to_all(field, ('chan', 'batch'), split_axis=0, concat_axis=2, til...]
    unnamed x39 -> x3, local copies, waits for them, and re-layouts: 39.6 us -> 7.89 us
    convert_element_type x5 -> x0, other arithmetic: 24.6 us -> none  [the longest x1 10.9 us: shards(): first = wide + mixed_back.astype(jnp.float32)]
    reshape x4 -> x0, local copies, waits for them, and re-layouts: 23.3 us -> none  [the longest x1 8.51 us: shards(): expand(hidden_act, tok_out, 0).astype(jnp.bfloat16)]
  transfers between devices with their start and end apart: 4 -> 0, of which waited for: 3 -> 0; matrix products, arithmetic and copies ran while one was open for 0% -> 0% of each run, Pallas kernels for 0% -> 0%
where the time goes in v1:
time: 115 us; the launch traced here: 114 us
  Pallas kernels  106 us (92%)
  local copies, waits for them, and re-layouts  7.89 us (7%)
    pallas_call x1, Pallas kernels, fused(): pl.pallas_call(kernel, out_shape=(jax.ShapeDtypeStruct((B, C, L), F32), j...  106 us
    unnamed x3, local copies, waits for them, and re-layouts  7.89 us

profile of v1, /device:TPU:1, one launch (start us, length us, event | category | flops | bytes accessed | tf_op | source)
XLA Modules:
  0.0 114.2 jit_solution(4442371326542135678)
XLA Ops:
  0.6 2.5 %copy.15 = bf16[256,16,128]{2,0,1:T(8,128)(2,1)} copy(bf16[256,16,128]{2,1,0:T(8,128)(2,1)} %param.10) | data formatting | bytes 2097152 | tf_op args[0]
  3.1 105.7 %shard_map.113 = (f32[16,256,128]{2,1,0:T(8,128)}, f32[8,256]{1,0:T(8,128)}) custom-call(bf16[16,256,128]{2,1,0:T(8,128)(2,1)} %bitcast.9, f32[1,256]{1,0:T(1,128)} %bitcast.13, bf16[2048,2048]{1,0:T(8,128)(2,1)} %win_hbm.1, bf16[2048,2048]{1,0:T(8,128)(2,1)} %wout_hbm.1, f32[1,256]{1,0:T(1,128)} %bitcast.14, bf16[256,1024]{1,0:T(8,128)(2,1)} %ci_hbm.1, ...), custom_call_target="tpu_custom_call" | custom-call | tf_op jit(solution)/shard_map/pallas_call | solution.py:465
  108.8 4.1 %copy.13 = f32[256,16,128]{2,1,0:T(8,128)} copy(f32[256,16,128]{2,0,1:T(8,128)} %bitcast.10) | data formatting | bytes 4194304
  112.9 1.3 %copy.17 = f32[256,8]{0,1:T(8,128)} copy(f32[256,8]{0,1:T(8,128)} %bitcast.11) | data formatting | bytes 16384

commit v2 on v1

--- a/solution.py
+++ b/solution.py
@@ -21,6 +21,8 @@
 NC = 2
 NB = B // NC
 R = NB * CL
+G = 8
+KB = 256
 Q = J // 8
 
 GELU_K = 0.7978845608028654
@@ -38,10 +40,9 @@
 
 def gelu_both(v):
     square = v * v
-    inner = jnp.tanh(v * (GELU_K + (GELU_K * GELU_C) * square))
-    half = 0.5 + 0.5 * inner
+    half = 0.5 + 0.5 * jnp.tanh(v * (GELU_K + (GELU_K * GELU_C) * square))
     value = v * half
-    slope = half + (0.5 * v) * (1.0 - inner * inner) * (GELU_K + (3.0 * GELU_K * GELU_C) * square)
+    slope = half + value * (1.0 - half) * (2.0 * GELU_K + (6.0 * GELU_K * GELU_C) * square)
     return value, slope
 
 
@@ -52,7 +53,7 @@
 def kernel(
     x_hbm, gin_ref, win_hbm, wout_hbm, gmid_ref, ci_hbm, co_hbm, head_ref, act_ref, ord_ref,
     out_hbm, hg_ref,
-    x_s, win, wout, ci, co, cit, cot, gin, gmid, head16, headc, tgt, mu, rstd, bf,
+    x_raw, x_s, win, wout, ci, co, cit, cot, gin, gmid, head16, headc, tgt, mu, rstd, bf,
     send1, send2, send3, send4, recv1, recv2, recv3, recv4,
     part1, part2, sibr1, sibr2, zs1, zs2, zr1, zr2, hact1, hact2, ownp, hslope,
     inner_s, slope_s, bip_s, hp, hbuf_a, hbuf_y, hbuf_x, hsend,
@@ -84,14 +85,13 @@
         return out
 
     loads = [
-        pltpu.make_async_copy(x_hbm, x_s, ld_sem.at[0]),
+        pltpu.make_async_copy(x_hbm, x_raw, ld_sem.at[0]),
         pltpu.make_async_copy(win_hbm, win, ld_sem.at[1]),
         pltpu.make_async_copy(ci_hbm, ci, ld_sem.at[2]),
         pltpu.make_async_copy(co_hbm, co, ld_sem.at[3]),
         pltpu.make_async_copy(wout_hbm, wout, ld_sem.at[4]),
     ]
-    for load in loads:
-        load.start()
+    loads[0].start()
 
     barrier = pltpu.get_barrier_semaphore()
     for i in range(1, NP):
@@ -104,23 +104,13 @@
         )
 
     gin[...] = jnp.transpose(jnp.broadcast_to(gin_ref[...], (L, C)))
-    gmid[...] = jnp.transpose(jnp.broadcast_to(gmid_ref[...], (L, C)))
-    head_rows = jnp.concatenate([head_ref[...].astype(F32), jnp.zeros((8, C), F32)], axis=0)
-    head16[...] = head_rows.astype(BF16)
-    wide_head = jnp.concatenate([head_rows, jnp.zeros((L - 16, C), F32)], axis=0)
-    headc[...] = jnp.transpose(wide_head)[:, :16].astype(BF16)
-    spot = lax.broadcasted_iota(jnp.int32, (L, L), 0) == lax.rem(ord_ref[...], L)
-    targets = mm(act_ref[...].astype(F32).astype(BF16), spot.astype(F32).astype(BF16))
-    for b in range(B):
-        tgt[b] = targets[b : b + 1, :]
-    hp[...] = jnp.zeros((16, C), F32)
 
     def a2a_copy(k, h, send, recv, p, slot):
         return pltpu.make_async_remote_copy(
             src_ref=send.at[p, pl.ds(h * NB, NB)],
             dst_ref=recv.at[h, slot],
-            send_sem=a2a_s.at[k, h, p],
-            recv_sem=a2a_r.at[k, h, slot],
+            send_sem=a2a_s.at[k, h],
+            recv_sem=a2a_r.at[k, h],
             device_id=plane(p),
             device_id_type=MESH,
         )
@@ -134,20 +124,12 @@
 
     def a2a_wait(k, h, send, recv):
         recv[h, me] = send[me, pl.ds(h * NB, NB)]
-
-        def body(i, carry):
-            p = lax.rem(me + i, NP)
-            a2a_copy(k, h, send, recv, p, p).wait_recv()
-            return carry
-
-        lax.fori_loop(1, NP, body, 0)
+        others = recv.at[h, pl.ds(0, NP - 1)]
+        pltpu.make_async_copy(others, others, a2a_r.at[k, h]).wait()
 
     def a2a_drain(k, h, send, recv):
-        def body(i, carry):
-            a2a_copy(k, h, send, recv, lax.rem(me + i, NP), me).wait_send()
-            return carry
-
-        lax.fori_loop(1, NP, body, 0)
+        others = recv.at[h, pl.ds(0, NP - 1)]
+        pltpu.make_async_copy(others, others, a2a_s.at[k, h]).wait()
 
     def sib_copy(s, h, part, sibr, i):
         return pltpu.make_async_remote_copy(
@@ -272,46 +254,49 @@
 
     def channel_part(h):
         def body(i, carry):
-            l0, l1 = 2 * i, 2 * i + 1
-            b0, b1 = h * NB + l0, h * NB + l1
-            wide = jnp.concatenate([x_s[b0], x_s[b1]], axis=1).astype(F32)
-            mixed = jnp.concatenate([recv2[h, :, l0].reshape(C, L), recv2[h, :, l1].reshape(C, L)], axis=1)
+            local = [G * i + g for g in range(G)]
+            at = [h * NB + b for b in local]
+
+            def lanes(pieces):
+                return jnp.concatenate(pieces, axis=1)
+
+            wide = lanes([x_s[b] for b in at]).astype(F32)
+            mixed = lanes([recv2[h, :, b].reshape(C, L) for b in local])
             first = wide + mixed.astype(F32)
-            gain = jnp.concatenate([gmid[...], gmid[...]], axis=1)
+            gain = lanes([gmid[...]] * G)
             center = mean0(first)
             unit = first - center
             scale = lax.rsqrt(mean0(unit * unit) + EPS)
             unit = unit * scale
             normed = (unit * gain).astype(BF16)
-            for kb in range(4):
-                block = slice(kb * 256, kb * 256 + 256)
+            for kb in range(K // KB):
+                block = slice(kb * KB, kb * KB + KB)
                 value, slope = gelu_both(mm(cit[block, :], normed))
                 inner_s[block, :] = value.astype(BF16)
                 slope_s[block, :] = slope
             second = (first + mm(cot[...], inner_s[...])).astype(BF16)
             logits = mm(head16[...], second)[:8]
-            target = jnp.concatenate([tgt[b0], tgt[b1]], axis=1)
-            phases = lax.broadcasted_iota(jnp.int32, (8, 2 * L), 0).astype(F32)
+            target = lanes([tgt[b] for b in at])
+            phases = lax.broadcasted_iota(jnp.int32, (8, G * L), 0).astype(F32)
             exps = jnp.exp(logits - jnp.max(logits, axis=0, keepdims=True))
             probs = exps / jnp.sum(exps, axis=0, keepdims=True)
             diff = probs - jnp.where(phases == target, 1.0, 0.0)
-            slope16 = jnp.concatenate([diff, jnp.zeros((8, 2 * L), F32)], axis=0).astype(BF16)
+            slope16 = jnp.concatenate([diff, jnp.zeros((8, G * L), F32)], axis=0).astype(BF16)
             hp[...] += mm_nt(slope16, second)
             back_second = mm(headc[...], slope16)
             back_low = back_second.astype(BF16)
-            for kb in range(4):
-                block = slice(kb * 256, kb * 256 + 256)
+            for kb in range(K // KB):
+                block = slice(kb * KB, kb * KB + KB)
                 bip_s[block, :] = (mm(co[block, :], back_low) * slope_s[block, :]).astype(BF16)
             w = mm(ci[...], bip_s[...]) * gain
             back = back_second + scale * (w - mean0(w) - unit * mean0(w * unit))
-            bf[b0] = back[:, :L]
-            bf[b1] = back[:, L:]
             low = back.astype(BF16)
-            send3[:, b0] = low[:, :L].reshape(NP, CL, L)
-            send3[:, b1] = low[:, L:].reshape(NP, CL, L)
-            return carry
-
-        lax.fori_loop(0, NB // 2, body, 0)
+            for g in range(G):
+                bf[at[g]] = back[:, g * L : (g + 1) * L]
+                send3[:, at[g]] = low[:, g * L : (g + 1) * L].reshape(NP, CL, L)
+            return carry
+
+        lax.fori_loop(0, NB // G, body, 0)
 
     def norm_back(h):
         def body(i, carry):
@@ -320,13 +305,23 @@
             unit = (x_s[b].astype(F32) - mu[b]) * scale
             w = recv4[h, :, i].reshape(C, L).astype(F32) * gin[...]
             bf[b] = bf[b] + scale * (w - mean0(w) - unit * mean0(w * unit))
+            out_copy(b).start()
             return carry
 
         lax.fori_loop(0, NB, body, 0)
 
-    def out_copy(h):
-        piece = pl.ds(h * NB, NB)
-        return pltpu.make_async_copy(bf.at[piece], out_hbm.at[piece], out_sem.at[h])
+    def out_copy(b):
+        return pltpu.make_async_copy(bf.at[b], out_hbm.at[:, b], out_sem.at[b])
+
+    def line_drain(s, h, part, sibr, zs, zr, hact):
+        for i in range(2):
+            sib_copy(s, h, part, sibr, i).wait_send()
+        for i in range(3):
+            z_copy(s, h, zs, zr, i, xor(z, 1), 0).wait_send()
+        for d in range(1, 4):
+            ag_copy(s, h, hact, d, mine).wait_send()
+        for zz in range(4):
+            fw_copy(s, h, hact, zz, core).wait_send()
 
     def ha_copy(i):
         return pltpu.make_async_remote_copy(
@@ -353,12 +348,38 @@
         return out
 
     loads[0].wait()
+
+    def samples_first(h):
+        def body(i, carry):
+            piece = pl.ds(pl.multiple_of(i * CL, CL), CL)
+            field = x_raw[piece].astype(F32)[:, h * NB : (h + 1) * NB]
+            x_s[h * NB : (h + 1) * NB, piece] = jnp.transpose(field, (1, 0, 2)).astype(BF16)
+            return carry
+
+        lax.fori_loop(0, NP, body, 0)
+
+    samples_first(0)
     norm_in(0)
     pl.semaphore_wait(barrier, NP - 1 + 7)
     a2a_send(0, 0, send1, recv1)
+    for load in loads[1:]:
+        load.start()
     for h in range(1, NC):
+        samples_first(h)
         norm_in(h)
+        a2a_drain(0, h - 1, send1, recv1)
         a2a_send(0, h, send1, recv1)
+    gmid[...] = jnp.transpose(jnp.broadcast_to(gmid_ref[...], (L, C)))
+    head_rows = jnp.concatenate([head_ref[...].astype(F32), jnp.zeros((8, C), F32)], axis=0)
+    head16[...] = head_rows.astype(BF16)
+    wide_head = jnp.concatenate([head_rows, jnp.zeros((L - 16, C), F32)], axis=0)
+    headc[...] = jnp.transpose(wide_head)[:, :16].astype(BF16)
+    spot = lax.broadcasted_iota(jnp.int32, (L, L), 0) == lax.rem(ord_ref[...], L)
+    targets = mm(act_ref[...].astype(F32).astype(BF16), spot.astype(F32).astype(BF16))
+    for b in range(B):
+        tgt[b] = targets[b : b + 1, :]
+    hp[...] = jnp.zeros((16, C), F32)
+
     loads[2].wait()
     loads[3].wait()
     for kb in range(4):
@@ -383,6 +404,10 @@
         a2a_wait(1, h, send2, recv2)
         channel_part(h)
         a2a_send(2, h, send3, recv3)
+    a2a_drain(0, NC - 1, send1, recv1)
+    for h in range(NC):
+        line_drain(0, h, part1, sibr1, zs1, zr1, hact1)
+        a2a_drain(1, h, send2, recv2)
     hsend[0] = hp[:8]
     hbuf_a[ag] = hp[:8]
     for i in range(1, 8):
@@ -415,25 +440,17 @@
         hx_copy(i).wait()
     hg_ref[...] = total(hbuf_x, 4) * (1.0 / (B * A))
     for h in range(NC):
+        a2a_drain(2, h, send3, recv3)
+        line_drain(1, h, part2, sibr2, zs2, zr2, hact2)
+        if h < NC - 1:
+            a2a_drain(3, h, send4, recv4)
+    for h in range(NC):
         a2a_wait(3, h, send4, recv4)
         norm_back(h)
-        out_copy(h).start()
-
-    for h in range(NC):
-        for k, (send, recv) in enumerate(((send1, recv1), (send2, recv2), (send3, recv3), (send4, recv4))):
-            a2a_drain(k, h, send, recv)
-        for s, (part, sibr, zs, zr, hact) in enumerate(
-            ((part1, sibr1, zs1, zr1, hact1), (part2, sibr2, zs2, zr2, hact2))
-        ):
-            for i in range(2):
-                sib_copy(s, h, part, sibr, i).wait_send()
-            for i in range(3):
-                z_copy(s, h, zs, zr, i, xor(z, 1), 0).wait_send()
-            for d in range(1, 4):
-                ag_copy(s, h, hact, d, mine).wait_send()
-            for zz in range(4):
-                fw_copy(s, h, hact, zz, core).wait_send()
-        out_copy(h).wait()
+
+    a2a_drain(3, NC - 1, send4, recv4)
+    for b in range(B):
+        out_copy(b).wait()
 
 
 def fused(x, gin, win, wout, gmid, ci, co, head, actions, order):
@@ -444,7 +461,7 @@
     exchange = V((NP, B, CL, L), BF16)
     arrive = V((NC, NP, NB, CL, L), BF16)
     scratch = [
-        V((B, C, L), BF16), V((T, J), BF16), V((J, T), BF16),
+        V((C, B, L), BF16), V((B, C, L), BF16), V((T, J), BF16), V((J, T), BF16),
         V((C, K), BF16), V((K, C), BF16), V((K, C), BF16), V((C, K), BF16),
         V((C, L), F32), V((C, L), F32), V((16, C), BF16), V((C, 16), BF16),
         V((B, 1, L), F32), V((B, 1, L), F32), V((B, 1, L), F32), V((B, C, L), F32),
@@ -455,16 +472,16 @@
         V((NC, 3, R, Q), BF16), V((NC, 3, R, Q), BF16),
         V((NC, 8, R, Q), BF16), V((NC, 8, R, Q), BF16),
         V((2, NC, 2, R, Q), F32), V((NC, R, Q), F32),
-        V((K, 2 * L), BF16), V((K, 2 * L), F32), V((K, 2 * L), BF16), V((16, C), F32),
+        V((K, G * L), BF16), V((K, G * L), F32), V((K, G * L), BF16), V((16, C), F32),
         V((8, 8, C), F32), V((4, 8, C), F32), V((4, 8, C), F32), V((3, 8, C), F32),
-        dma((5,)), dma((NC,)), dma((4, NC, NP)), dma((4, NC, NP)),
+        dma((5,)), dma((B,)), dma((4, NC)), dma((4, NC)),
         dma((2, NC, 2)), dma((2, NC, 2)), dma((2, NC, 3)), dma((2, NC, 3)),
         dma((2, NC, 3)), dma((2, NC, 3)), dma((2, NC, 4)), dma((2, NC, 4)),
         dma((8,)), dma((8,)), dma((4,)), dma((4,)), dma((4,)), dma((4,)),
     ]
     return pl.pallas_call(
         kernel,
-        out_shape=(jax.ShapeDtypeStruct((B, C, L), F32), jax.ShapeDtypeStruct((8, C), F32)),
+        out_shape=(jax.ShapeDtypeStruct((C, B, L), F32), jax.ShapeDtypeStruct((8, C), F32)),
         in_specs=[hbm, vmem, hbm, hbm, vmem, hbm, hbm, vmem, vmem, vmem],
         out_specs=(hbm, vmem),
         scratch_shapes=scratch,
@@ -476,7 +493,7 @@
 
 def shards(features, norm_gain, tok_in, tok_out, mix_gain, chan_in, chan_out, head, actions, order):
     grad, head_grad = fused(
-        jnp.transpose(features, (1, 0, 2)),
+        features,
         norm_gain.reshape(1, C),
         tok_in,
         tok_out,
@@ -487,7 +504,7 @@
         actions,
         order.reshape(1, L),
     )
-    return jnp.transpose(grad, (1, 0, 2)), head_grad.T
+    return grad, head_grad.T
 
 
 def solution(mesh):

time: 115 us -> 101 us (0.88)
  Pallas kernels: 106 us -> 95.8 us
  local copies, waits for them, and re-layouts: 7.89 us -> 4.34 us
    pallas_call x1, Pallas kernels: 106 us -> 95.8 us  [fused(): pl.pallas_call(kernel, out_shape=(jax.ShapeDtypeStruct((C, B, L), F32), j...]
    unnamed x3 -> x2, local copies, waits for them, and re-layouts: 7.89 us -> 4.34 us
where the time goes in v2:
time: 101 us
  Pallas kernels  95.8 us (95%)
  local copies, waits for them, and re-layouts  4.34 us (4%)
    pallas_call x1, Pallas kernels, fused(): pl.pallas_call(kernel, out_shape=(jax.ShapeDtypeStruct((C, B, L), F32), j...  95.8 us
    unnamed x2, local copies, waits for them, and re-layouts  4.34 us

profile of v2, /device:TPU:1, one launch (start us, length us, event | category | flops | bytes accessed | tf_op | source)
XLA Modules:
  0.0 100.8 jit_solution(15392259754494296230)
XLA Ops:
  0.6 95.8 %shard_map.113 = (f32[256,16,128]{2,1,0:T(8,128)}, f32[8,256]{1,0:T(8,128)}) custom-call(bf16[256,16,128]{2,1,0:T(8,128)(2,1)} %x_hbm.1, f32[1,256]{1,0:T(1,128)} %bitcast.7, bf16[2048,2048]{1,0:T(8,128)(2,1)} %win_hbm.1, bf16[2048,2048]{1,0:T(8,128)(2,1)} %wout_hbm.1, f32[1,256]{1,0:T(1,128)} %bitcast.8, bf16[256,1024]{1,0:T(8,128)(2,1)} %ci_hbm.1, ...), custom_call_target="tpu_custom_call" | custom-call | tf_op jit(solution)/shard_map/pallas_call | solution.py:482
  96.5 3.0 %copy.14 = f32[256,16,128]{2,1,0:T(8,128)} copy(f32[256,16,128]{2,1,0:T(8,128)} %get-tuple-element.8) | data formatting | bytes 4194304
  99.5 1.3 %copy.15 = f32[256,8]{0,1:T(8,128)} copy(f32[256,8]{0,1:T(8,128)} %bitcast.5) | data formatting | bytes 16384

commit v3 on v2

--- a/solution.py
+++ b/solution.py
@@ -21,8 +21,9 @@
 NC = 2
 NB = B // NC
 R = NB * CL
-G = 8
+G = 4
 KB = 256
+PIECES = 8
 Q = J // 8
 
 GELU_K = 0.7978845608028654
@@ -122,6 +123,21 @@
 
         lax.fori_loop(1, NP, body, 0)
 
+    def send_step(k, h, i, send, recv):
+        def body(d, carry):
+            p = lax.rem(me + d, NP)
+            pltpu.make_async_remote_copy(
+                src_ref=send.at[p, pl.ds(h * NB + i * G, G)],
+                dst_ref=recv.at[h, me, pl.ds(i * G, G)],
+                send_sem=a2a_s.at[k, h],
+                recv_sem=a2a_r.at[k, h],
+                device_id=plane(p),
+                device_id_type=MESH,
+            ).start()
+            return carry
+
+        lax.fori_loop(1, NP, body, 0)
+
     def a2a_wait(k, h, send, recv):
         recv[h, me] = send[me, pl.ds(h * NB, NB)]
         others = recv.at[h, pl.ds(0, NP - 1)]
@@ -238,9 +254,9 @@
     def rows(w, block):
         return w[pl.ds(pl.multiple_of(block * Q, Q), 2 * Q), :]
 
-    def norm_in(h):
+    def norm_in(first, count):
         def body(i, carry):
-            b = h * NB + i
+            b = first + i
             field = x_s[b].astype(F32)
             center = mean0(field)
             field = field - center
@@ -250,7 +266,7 @@
             send1[:, b] = (field * scale * gin[...]).astype(BF16).reshape(NP, CL, L)
             return carry
 
-        lax.fori_loop(0, NB, body, 0)
+        lax.fori_loop(0, count, body, 0)
 
     def channel_part(h):
         def body(i, carry):
@@ -294,6 +310,8 @@
             for g in range(G):
                 bf[at[g]] = back[:, g * L : (g + 1) * L]
                 send3[:, at[g]] = low[:, g * L : (g + 1) * L].reshape(NP, CL, L)
+
+            send_step(2, h, i, send3, recv3)
             return carry
 
         lax.fori_loop(0, NB // G, body, 0)
@@ -348,25 +366,30 @@
         return out
 
     loads[0].wait()
-
-    def samples_first(h):
+    loads[1].start()
+
+    def samples_first(first, count):
         def body(i, carry):
             piece = pl.ds(pl.multiple_of(i * CL, CL), CL)
-            field = x_raw[piece].astype(F32)[:, h * NB : (h + 1) * NB]
-            x_s[h * NB : (h + 1) * NB, piece] = jnp.transpose(field, (1, 0, 2)).astype(BF16)
+            field = x_raw[piece].astype(F32)[:, first : first + count]
+            x_s[first : first + count, piece] = jnp.transpose(field, (1, 0, 2)).astype(BF16)
             return carry
 
         lax.fori_loop(0, NP, body, 0)
 
-    samples_first(0)
-    norm_in(0)
+    samples_first(0, G)
+    norm_in(0, G)
     pl.semaphore_wait(barrier, NP - 1 + 7)
-    a2a_send(0, 0, send1, recv1)
-    for load in loads[1:]:
-        load.start()
+    send_step(0, 0, 0, send1, recv1)
+    for i in range(1, NB // G):
+        samples_first(i * G, G)
+        norm_in(i * G, G)
+        send_step(0, 0, i, send1, recv1)
+    loads[2].start()
+    loads[3].start()
     for h in range(1, NC):
-        samples_first(h)
-        norm_in(h)
+        samples_first(h * NB, NB)
+        norm_in(h * NB, NB)
         a2a_drain(0, h - 1, send1, recv1)
         a2a_send(0, h, send1, recv1)
     gmid[...] = jnp.transpose(jnp.broadcast_to(gmid_ref[...], (L, C)))
@@ -387,6 +410,7 @@
         cit[block, :] = jnp.transpose(ci[:, block])
         cot[:, block] = jnp.transpose(co[block, :])
     loads[1].wait()
+    loads[4].start()
     for h in range(NC):
         a2a_wait(0, h, send1, recv1)
         contract(0, h, recv1, lambda a, block: mm(a, cols(win, block)), part1, sibr1, zs1, zr1)
@@ -403,7 +427,6 @@
     for h in range(NC):
         a2a_wait(1, h, send2, recv2)
         channel_part(h)
-        a2a_send(2, h, send3, recv3)
     a2a_drain(0, NC - 1, send1, recv1)
     for h in range(NC):
         line_drain(0, h, part1, sibr1, zs1, zr1, hact1)
@@ -438,7 +461,7 @@
         expand(3, h, hact2, lambda a, group: mm_nt(a, rows(win, group * 2)), send4, recv4)
     for i in range(1, 4):
         hx_copy(i).wait()
-    hg_ref[...] = total(hbuf_x, 4) * (1.0 / (B * A))
+    hg_ref[...] = total(hbuf_x, 4)
     for h in range(NC):
         a2a_drain(2, h, send3, recv3)
         line_drain(1, h, part2, sibr2, zs2, zr2, hact2)
@@ -491,6 +514,43 @@
     )(x, gin, win, wout, gmid, ci, co, head, actions, order)
 
 
+def hand_over(grad_in, head_in, grad_out, head_out, held, in_sem, out_sem):
+    def piece(i):
+        return pl.ds(i * (C // PIECES), C // PIECES)
+
+    arrive = [
+        pltpu.make_async_copy(grad_in.at[piece(i)], held.at[piece(i)], in_sem.at[i]) for i in range(PIECES)
+    ]
+    leave = [
+        pltpu.make_async_copy(held.at[piece(i)], grad_out.at[piece(i)], out_sem.at[i]) for i in range(PIECES)
+    ]
+    for copy in arrive:
+        copy.start()
+    head_out[...] = head_in[...] * (1.0 / (B * A))
+    for i in range(PIECES):
+        arrive[i].wait()
+        leave[i].start()
+    for copy in leave:
+        copy.wait()
+
+
+def deliver(grad, head):
+    hbm = pl.BlockSpec(memory_space=pl.ANY)
+    vmem = pl.BlockSpec(memory_space=pltpu.VMEM)
+    return pl.pallas_call(
+        hand_over,
+        out_shape=(jax.ShapeDtypeStruct((C, B, L), F32), jax.ShapeDtypeStruct((8, C), F32)),
+        in_specs=[hbm, vmem],
+        out_specs=(hbm, vmem),
+        scratch_shapes=[
+            pltpu.VMEM((C, B, L), F32),
+            pltpu.SemaphoreType.DMA((PIECES,)),
+            pltpu.SemaphoreType.DMA((PIECES,)),
+        ],
+        compiler_params=pltpu.CompilerParams(vmem_limit_bytes=60 << 20),
+    )(grad, head)
+
+
 def shards(features, norm_gain, tok_in, tok_out, mix_gain, chan_in, chan_out, head, actions, order):
     grad, head_grad = fused(
         features,
@@ -504,6 +564,7 @@
         actions,
         order.reshape(1, L),
     )
+    grad, head_grad = deliver(grad, head_grad)
     return grad, head_grad.T
 
 

time: 101 us -> 99.8 us (0.988)
  local copies, waits for them, and re-layouts: 4.34 us -> 0 us
  Pallas kernels: 95.8 us -> 98.7 us
    unnamed x2 -> x0, local copies, waits for them, and re-layouts: 4.34 us -> none
    pallas_call x0 -> x1, Pallas kernels: none -> 3.69 us  [deliver(): pl.pallas_call(hand_over, out_shape=(jax.ShapeDtypeStruct((C, B, L), F32)...]
where the time goes in v3:
time: 99.8 us; the launch traced here: 99.5 us
  Pallas kernels  98.7 us (99%)
    pallas_call x1, Pallas kernels, fused(): pl.pallas_call(kernel, out_shape=(jax.ShapeDtypeStruct((C, B, L), F32), j...  95 us
    pallas_call x1, Pallas kernels, deliver(): pl.pallas_call(hand_over, out_shape=(jax.ShapeDtypeStruct((C, B, L), F32)...  3.69 us

profile of v3, /device:TPU:1, one launch (start us, length us, event | category | flops | bytes accessed | tf_op | source)
XLA Modules:
  0.0 99.5 jit_solution(942910483472799842)
XLA Ops:
  0.6 95.0 %shard_map.113 = (f32[256,16,128]{2,1,0:T(8,128)}, f32[8,256]{1,0:T(8,128)}) custom-call(bf16[256,16,128]{2,1,0:T(8,128)(2,1)} %x_hbm.1, f32[1,256]{1,0:T(1,128)} %bitcast.6, bf16[2048,2048]{1,0:T(8,128)(2,1)} %win_hbm.1, bf16[2048,2048]{1,0:T(8,128)(2,1)} %wout_hbm.1, f32[1,256]{1,0:T(1,128)} %bitcast.7, bf16[256,1024]{1,0:T(8,128)(2,1)} %ci_hbm.1, ...), custom_call_target="tpu_custom_call" | custom-call | tf_op jit(solution)/shard_map/pallas_call | solution.py:505
  95.7 3.7 %shard_map.114 = (f32[256,16,128]{2,1,0:T(8,128)}, f32[8,256]{1,0:T(8,128)}) custom-call(f32[256,16,128]{2,1,0:T(8,128)} %get-tuple-element.6.grad_in, f32[8,256]{1,0:T(8,128)} %get-tuple-element.7.head_in), custom_call_target="tpu_custom_call" | custom-call | tf_op jit(solution)/shard_map/pallas_call | solution.py:540

commit v4 on v3

--- a/solution.py
+++ b/solution.py
@@ -52,9 +52,9 @@
 
 
 def kernel(
-    x_hbm, gin_ref, win_hbm, wout_hbm, gmid_ref, ci_hbm, co_hbm, head_ref, act_ref, ord_ref,
+    x_hbm, gin_hbm, win_hbm, wout_hbm, gmid_hbm, ci_hbm, co_hbm, head_hbm, act_hbm, ord_hbm,
     out_hbm, hg_ref,
-    x_raw, x_s, win, wout, ci, co, cit, cot, gin, gmid, head16, headc, tgt, mu, rstd, bf,
+    gin_ref, gmid_ref, head_ref, act_ref, ord_ref, x_raw, x_s, win, wout, ci, co, cit, cot, gin, gmid, head16, headc, tgt, mu, rstd, bf,
     send1, send2, send3, send4, recv1, recv2, recv3, recv4,
     part1, part2, sibr1, sibr2, zs1, zs2, zr1, zr2, hact1, hact2, ownp, hslope,
     inner_s, slope_s, bip_s, hp, hbuf_a, hbuf_y, hbuf_x, hsend,
@@ -91,8 +91,16 @@
         pltpu.make_async_copy(ci_hbm, ci, ld_sem.at[2]),
         pltpu.make_async_copy(co_hbm, co, ld_sem.at[3]),
         pltpu.make_async_copy(wout_hbm, wout, ld_sem.at[4]),
+        pltpu.make_async_copy(gin_hbm, gin_ref, ld_sem.at[5]),
+        pltpu.make_async_copy(gmid_hbm, gmid_ref, ld_sem.at[6]),
+        pltpu.make_async_copy(head_hbm, head_ref, ld_sem.at[7]),
+        pltpu.make_async_copy(act_hbm, act_ref, ld_sem.at[8]),
+        pltpu.make_async_copy(ord_hbm, ord_ref, ld_sem.at[9]),
     ]
+    loads[5].start()
     loads[0].start()
+    for load in loads[6:]:
+        load.start()
 
     barrier = pltpu.get_barrier_semaphore()
     for i in range(1, NP):
@@ -104,6 +112,7 @@
             device_id_type=MESH,
         )
 
+    loads[5].wait()
     gin[...] = jnp.transpose(jnp.broadcast_to(gin_ref[...], (L, C)))
 
     def a2a_copy(k, h, send, recv, p, slot):
@@ -392,6 +401,8 @@
         norm_in(h * NB, NB)
         a2a_drain(0, h - 1, send1, recv1)
         a2a_send(0, h, send1, recv1)
+    for load in loads[6:]:
+        load.wait()
     gmid[...] = jnp.transpose(jnp.broadcast_to(gmid_ref[...], (L, C)))
     head_rows = jnp.concatenate([head_ref[...].astype(F32), jnp.zeros((8, C), F32)], axis=0)
     head16[...] = head_rows.astype(BF16)
@@ -484,6 +495,7 @@
     exchange = V((NP, B, CL, L), BF16)
     arrive = V((NC, NP, NB, CL, L), BF16)
     scratch = [
+        V((1, C), F32), V((1, C), F32), V((8, C), BF16), V((B, L), jnp.int32), V((1, L), jnp.int32),
         V((C, B, L), BF16), V((B, C, L), BF16), V((T, J), BF16), V((J, T), BF16),
         V((C, K), BF16), V((K, C), BF16), V((K, C), BF16), V((C, K), BF16),
         V((C, L), F32), V((C, L), F32), V((16, C), BF16), V((C, 16), BF16),
@@ -497,7 +509,7 @@
         V((2, NC, 2, R, Q), F32), V((NC, R, Q), F32),
         V((K, G * L), BF16), V((K, G * L), F32), V((K, G * L), BF16), V((16, C), F32),
         V((8, 8, C), F32), V((4, 8, C), F32), V((4, 8, C), F32), V((3, 8, C), F32),
-        dma((5,)), dma((B,)), dma((4, NC)), dma((4, NC)),
+        dma((10,)), dma((B,)), dma((4, NC)), dma((4, NC)),
         dma((2, NC, 2)), dma((2, NC, 2)), dma((2, NC, 3)), dma((2, NC, 3)),
         dma((2, NC, 3)), dma((2, NC, 3)), dma((2, NC, 4)), dma((2, NC, 4)),
         dma((8,)), dma((8,)), dma((4,)), dma((4,)), dma((4,)), dma((4,)),
@@ -505,32 +517,23 @@
     return pl.pallas_call(
         kernel,
         out_shape=(jax.ShapeDtypeStruct((C, B, L), F32), jax.ShapeDtypeStruct((8, C), F32)),
-        in_specs=[hbm, vmem, hbm, hbm, vmem, hbm, hbm, vmem, vmem, vmem],
+        in_specs=[pl.BlockSpec(memory_space=pltpu.HBM)] * 10,
         out_specs=(hbm, vmem),
         scratch_shapes=scratch,
         compiler_params=pltpu.CompilerParams(
-            collective_id=0, has_side_effects=True, vmem_limit_bytes=58 << 20
+            collective_id=0, has_side_effects=True, vmem_limit_bytes=46 << 20
         ),
-    )(x, gin, win, wout, gmid, ci, co, head, actions, order)
-
-
-def hand_over(grad_in, head_in, grad_out, head_out, held, in_sem, out_sem):
-    def piece(i):
-        return pl.ds(i * (C // PIECES), C // PIECES)
-
-    arrive = [
-        pltpu.make_async_copy(grad_in.at[piece(i)], held.at[piece(i)], in_sem.at[i]) for i in range(PIECES)
-    ]
-    leave = [
-        pltpu.make_async_copy(held.at[piece(i)], grad_out.at[piece(i)], out_sem.at[i]) for i in range(PIECES)
-    ]
-    for copy in arrive:
-        copy.start()
+    )(*[pltpu.with_memory_space_constraint(v, pltpu.HBM) for v in (x, gin, win, wout, gmid, ci, co, head, actions, order)])
+
+
+def hand_over(grad_in, head_in, grad_out, head_out, sem):
+    copies = []
+    for i in range(PIECES):
+        piece = pl.ds(i * (C // PIECES), C // PIECES)
+        copies.append(pltpu.make_async_copy(grad_in.at[piece], grad_out.at[piece], sem.at[i]))
+        copies[-1].start()
     head_out[...] = head_in[...] * (1.0 / (B * A))
-    for i in range(PIECES):
-        arrive[i].wait()
-        leave[i].start()
-    for copy in leave:
+    for copy in copies:
         copy.wait()
 
 
@@ -542,12 +545,8 @@
         out_shape=(jax.ShapeDtypeStruct((C, B, L), F32), jax.ShapeDtypeStruct((8, C), F32)),
         in_specs=[hbm, vmem],
         out_specs=(hbm, vmem),
-        scratch_shapes=[
-            pltpu.VMEM((C, B, L), F32),
-            pltpu.SemaphoreType.DMA((PIECES,)),
-            pltpu.SemaphoreType.DMA((PIECES,)),
-        ],
-        compiler_params=pltpu.CompilerParams(vmem_limit_bytes=60 << 20),
+        scratch_shapes=[pltpu.SemaphoreType.DMA((PIECES,))],
+        compiler_params=pltpu.CompilerParams(vmem_limit_bytes=8 << 20),
     )(grad, head)
 
 

time: 99.8 us -> 97.2 us (0.974)
  Pallas kernels: 98.7 us -> 96.2 us
    pallas_call x1, Pallas kernels: 3.69 us -> 1.97 us  [deliver(): pl.pallas_call(hand_over, out_shape=(jax.ShapeDtypeStruct((C, B, L), F32)...]
where the time goes in v4:
time: 97.2 us; the launch traced here: 97 us
  Pallas kernels  96.2 us (99%)
    pallas_call x1, Pallas kernels, fused(): pl.pallas_call(kernel, out_shape=(jax.ShapeDtypeStruct((C, B, L), F32), j...  94.3 us
    pallas_call x1, Pallas kernels, deliver(): pl.pallas_call(hand_over, out_shape=(jax.ShapeDtypeStruct((C, B, L), F32)...  1.97 us

profile of v4, /device:TPU:1, one launch (start us, length us, event | category | flops | bytes accessed | tf_op | source)
XLA Modules:
  0.0 97.0 jit_solution(6281215797309091677)
XLA Ops:
  0.6 94.3 %shard_map.113 = (f32[256,16,128]{2,1,0:T(8,128)S(1)}, f32[8,256]{1,0:T(8,128)S(1)}) custom-call(bf16[256,16,128]{2,1,0:T(8,128)(2,1)} %x_hbm.1, f32[1,256]{1,0:T(1,128)} %bitcast.6, bf16[2048,2048]{1,0:T(8,128)(2,1)} %win_hbm.1, bf16[2048,2048]{1,0:T(8,128)(2,1)} %wout_hbm.1, f32[1,256]{1,0:T(1,128)} %bitcast.7, bf16[256,1024]{1,0:T(8,128)(2,1)} %ci_hbm.1, ...), custom_call_target="tpu_custom_call" | custom-call | tf_op jit(solution)/shard_map/pallas_call | solution.py:517
  94.9 2.0 %shard_map.114 = (f32[256,16,128]{2,1,0:T(8,128)}, f32[8,256]{1,0:T(8,128)}) custom-call(f32[256,16,128]{2,1,0:T(8,128)S(1)} %get-tuple-element.6.grad_in, f32[8,256]{1,0:T(8,128)S(1)} %get-tuple-element.7.head_in), custom_call_target="tpu_custom_call" | custom-call | tf_op jit(solution)/shard_map/pallas_call | solution.py:543

commit v5 on v4

--- a/solution.py
+++ b/solution.py
@@ -188,14 +188,11 @@
         return jnp.concatenate([recv[h, p].reshape(R, L) for p in range(NP)], axis=1)
 
     def contract(s, h, recv, product, part, sibr, zs, zr):
-        def for_sibling(i, carry):
+        half = z // 2
+        other = 1 - half
+        for i in (other, half):
             part[h, i] = product(rows_of(recv, h), (1 - core) * 4 + 2 * i).astype(BF16)
             sib_copy(s, h, part, sibr, i).start()
-            return carry
-
-        lax.fori_loop(0, 2, for_sibling, 0)
-        half = z // 2
-        other = 1 - half
         far = product(rows_of(recv, h), core * 4 + 2 * other)
         sib_copy(s, h, part, sibr, other).wait_recv()
         far = far + sibr[h, other].astype(F32)

time: 97.2 us -> 97.3 us (level)
  no operation moved by 1% of the time
where the time goes in v5:
time: 97.3 us; the launch traced here: 97.2 us
  Pallas kernels  96.4 us (99%)
    pallas_call x1, Pallas kernels, fused(): pl.pallas_call(kernel, out_shape=(jax.ShapeDtypeStruct((C, B, L), F32), j...  94.4 us
    pallas_call x1, Pallas kernels, deliver(): pl.pallas_call(hand_over, out_shape=(jax.ShapeDtypeStruct((C, B, L), F32)...  1.97 us

profile of v5, /device:TPU:1, one launch (start us, length us, event | category | flops | bytes accessed | tf_op | source)
XLA Modules:
  0.0 97.2 jit_solution(9914052736327896045)
XLA Ops:
  0.6 94.4 %shard_map.113 = (f32[256,16,128]{2,1,0:T(8,128)S(1)}, f32[8,256]{1,0:T(8,128)S(1)}) custom-call(bf16[256,16,128]{2,1,0:T(8,128)(2,1)} %x_hbm.1, f32[1,256]{1,0:T(1,128)} %bitcast.6, bf16[2048,2048]{1,0:T(8,128)(2,1)} %win_hbm.1, bf16[2048,2048]{1,0:T(8,128)(2,1)} %wout_hbm.1, f32[1,256]{1,0:T(1,128)} %bitcast.7, bf16[256,1024]{1,0:T(8,128)(2,1)} %ci_hbm.1, ...), custom_call_target="tpu_custom_call" | custom-call | tf_op jit(solution)/shard_map/pallas_call | solution.py:514
  95.1 2.0 %shard_map.114 = (f32[256,16,128]{2,1,0:T(8,128)}, f32[8,256]{1,0:T(8,128)}) custom-call(f32[256,16,128]{2,1,0:T(8,128)S(1)} %get-tuple-element.6.grad_in, f32[8,256]{1,0:T(8,128)S(1)} %get-tuple-element.7.head_in), custom_call_target="tpu_custom_call" | custom-call | tf_op jit(solution)/shard_map/pallas_call | solution.py:540
